TPU v7x, 256 devices: a whole 4x4x8 slice. The times are simulated.
256 devices in a mesh: seq: 64 (over y, x, z_hi, core), fsdp: 4 (over z_lo).
Axes of the slice: x: 4, y: 4, z: 8 (z_hi: 2, z_lo: 4; z = z_hi * 4 + z_lo), core: 2. Of those that a mesh axis runs over, the one named last changes fastest.
Arguments:
- tokens: bfloat16 [40960, 5120], P('seq', 'fsdp'), may hold values from -24 to 24
- w_local: bfloat16 [5120, 3, 1536], P('seq', None, 'fsdp'), may hold values from -0.078125 to 0.078125
- w_strided: bfloat16 [5120, 3, 1024], P('seq', None, 'fsdp'), may hold values from -0.078125 to 0.078125
- valid: int32 [64, 640], P('seq'), may hold values 0 or 1
- band_reach: int32 [12], P('fsdp'), may hold values from 1 to 4, as said below
Outputs:
- out_local: bfloat16 [40960, 1536], P('seq', 'fsdp')
- out_strided: bfloat16 [40960, 1024], P('seq', 'fsdp')
Inputs may be any that keep to these rules, and one draw needn't show every extreme that they name: Query block b of local head h sees band blocks b - band_reach[h] to b.
All inputs are finite; a program needn't handle non-finite values. No bound on the sum of `valid` on one device may be relied on, other than what follows from the above.
Results may differ from a plain program's by a relative error of at most 0.012.
The roundings to bfloat16 on the way count: a program that leaves them out, or rounds other values in their place, can miss the bound.
Values may be sent and summed in bfloat16 or wider, within the bound.
No kernel may reach another device: no remote copies, remote signals or barrier semaphores. Data moves between devices by JAX's collectives and lax.ppermute only.
A program may use at most 128 MiB of HBM per device.

v0:
```python
import math
import jax
import jax.numpy as jnp
from jax import lax
from jax.sharding import PartitionSpec as P

HD = 128
BLK = 128


def local_attend(qkv_day, valid_day, reach, head_size):
    query = qkv_day[:, 0]
    keys = qkv_day[:, 1]
    values = qkv_day[:, 2]
    seconds = qkv_day.shape[0]
    scores = jnp.einsum(
        "qhc,khc->hqk", query, keys, preferred_element_type=jnp.float32
    ) / math.sqrt(head_size)
    position = jnp.arange(seconds)
    causal = position[None, :] <= position[:, None]
    block = position // BLK
    band = block[None, None, :] >= block[None, :, None] - reach[:, None, None]
    seen = (valid_day[None, :] > 0) | (position[None, :] == position[:, None])
    allowed = causal[None] & band & seen[None]
    scores = jnp.where(allowed, scores, -jnp.inf)
    row_max = jnp.max(scores, axis=-1, keepdims=True)
    expo = jnp.exp(scores - row_max)
    probs = (expo / jnp.sum(expo, axis=-1, keepdims=True)).astype(jnp.bfloat16)
    result = jnp.einsum("hqk,khc->qhc", probs, values, preferred_element_type=jnp.float32)
    return result.astype(jnp.bfloat16).reshape(seconds, -1)


def body(tokens, w_local, w_strided, valid, band_reach):
    gathered = lax.all_gather(tokens, "fsdp", axis=1, tiled=True)
    seconds = gathered.shape[0]
    local_cols = w_local.shape[2]
    strided_cols = w_strided.shape[2]
    head_size = HD
    peers = lax.axis_size("seq")
    per_peer = seconds // peers

    def add_rows(piece):
        rows = piece.shape[0]
        return jnp.dot(gathered, piece.reshape(rows, -1), preferred_element_type=jnp.float32)

    acc_local = add_rows(lax.all_gather(w_local, "seq", axis=0, tiled=True))
    acc_strided = add_rows(lax.all_gather(w_strided, "seq", axis=0, tiled=True))
    packed = acc_strided.astype(jnp.bfloat16).reshape(1, peers, per_peer, 3 * strided_cols)
    marks = valid.astype(jnp.bfloat16).reshape(1, peers, per_peer)
    strided_packed = lax.all_to_all(packed, "seq", split_axis=1, concat_axis=0, tiled=True)
    strided_marks = lax.all_to_all(marks, "seq", split_axis=1, concat_axis=0, tiled=True)
    days = strided_packed.shape[0]
    count = strided_packed.shape[2]
    heads = strided_cols // head_size
    split_up = strided_packed.reshape(days, count, 3, heads, head_size)
    query = split_up[:, :, 0]
    keys = split_up[:, :, 1]
    values = split_up[:, :, 2]
    scores = jnp.einsum(
        "dshc,eshc->shde", query, keys, preferred_element_type=jnp.float32
    ) / math.sqrt(head_size)
    day = jnp.arange(days)
    causal = day[None, :] <= day[:, None]
    same = day[None, :] == day[:, None]
    seen = jnp.transpose(strided_marks[:, 0, :]) > 0
    allowed = causal[None, None] & (seen[:, None, None, :] | same[None, None])
    scores = jnp.where(allowed, scores, -jnp.inf)
    row_max = jnp.max(scores, axis=-1, keepdims=True)
    expo = jnp.exp(scores - row_max)
    probs = (expo / jnp.sum(expo, axis=-1, keepdims=True)).astype(jnp.bfloat16)
    result = jnp.einsum("shde,eshc->dshc", probs, values, preferred_element_type=jnp.float32)
    result = result.astype(jnp.bfloat16).reshape(days, 1, count, strided_cols)
    result = lax.all_to_all(result, "seq", split_axis=0, concat_axis=1, tiled=True)
    out_strided = result.reshape(seconds, strided_cols)
    qkv_local = acc_local.astype(jnp.bfloat16).reshape(
        seconds, 3, local_cols // head_size, head_size
    )
    out_local = local_attend(qkv_local, valid[0], band_reach, head_size)
    return (out_local, out_strided)


def solution(mesh):
    in_specs = (
        P("seq", "fsdp"),
        P("seq", None, "fsdp"),
        P("seq", None, "fsdp"),
        P("seq", None),
        P("fsdp"),
    )
    out_specs = (P("seq", "fsdp"), P("seq", "fsdp"))
    return jax.shard_map(body, mesh=mesh, in_specs=in_specs, out_specs=out_specs, check_vma=False)
```

profile of v0, /device:TPU:1, one launch (start us, length us, event | category | flops | bytes accessed | tf_op | source)
XLA Modules:
  0.0 441.7 jit_solution(410772100073191428)
XLA Ops:
  7.2 0.7 all-gather.8.cloned.1.call-update
  7.9 0.7 all-gather.4.cloned.1.call-update
  8.7 0.7 all-gather.6.cloned.1.call-update
  9.4 0.7 convert_reduce_fusion
  10.1 0.8 reshape.195
  10.9 15.6 %all-to-all-start.1 = ((bf16[1,64,10]{2,0,1:T(2,128)(2,1)}), bf16[1,64,10]{2,0,1:T(2,128)(2,1)S(1)}, u32[]{:S(2)}, u32[]{:S(2)}) async-start(bf16[1,64,10]{2,0,1:T(2,128)(2,1)} %reshape.195), calls=%async_computation.1 | async-start | bytes 65536 | tf_op jit(solution)/shard_map/all_to_all | solution.py:51
  26.5 100.5 %all-gather.8.cloned.1.call-done = bf16[5120,3,256]{2,0,1:T(8,128)(2,1)} async-done(((bf16[80,3,256]{2,0,1:T(8,128)(2,1)}), bf16[5120,3,256]{2,0,1:T(8,128)(2,1)}) %all-gather.8.cloned.1.call-update) | async-done | bytes 7864336 | tf_op jit(solution)/shard_map/all_gather | solution.py:47
  127.0 11.0 %copy.51 = bf16[5120,3,256]{0,2,1:T(8,128)(2,1)} copy(bf16[5120,3,256]{2,0,1:T(8,128)(2,1)} %all-gather.8.cloned.1.call-done) | data formatting | bytes 15728640 | tf_op jit(solution)/shard_map/all_gather | solution.py:47
  138.0 107.3 %all-gather.4.cloned.1.call-done = bf16[640,5120]{1,0:T(8,128)(2,1)} async-done(((bf16[640,1280]{1,0:T(8,128)(2,1)}), bf16[640,5120]{1,0:T(8,128)(2,1)}) %all-gather.4.cloned.1.call-update) | async-done | bytes 6553616 | tf_op jit(solution)/shard_map/all_gather | solution.py:34
  245.3 9.7 %convolution_convert_fusion.1 = bf16[640,768]{1,0:T(8,128)(2,1)S(1)} fusion(bf16[640,5120]{1,0:T(8,128)(2,1)} %all-gather.4.cloned.1.call-done, bf16[5120,768]{0,1:T(8,128)(2,1)} %bitcast.60), kind=kOutput, calls=%fused_computation.17 | convolution fusion | flops 5033656320 | bytes 15400960 | tf_op jit(solution)/shard_map/dot_general | solution.py:44
  255.0 1.4 reshape.189
  256.4 11.4 %all-to-all-start = ((bf16[1,64,10,768]{3,2,0,1:T(8,128)(2,1)}), bf16[1,64,10,768]{3,2,0,1:T(8,128)(2,1)S(1)}, u32[]{:S(2)}, u32[]{:S(2)}) async-start(bf16[1,64,10,768]{3,2,0,1:T(8,128)(2,1)} %bitcast.8), calls=%async_computation | async-start | bytes 3145728 | tf_op jit(solution)/shard_map/all_to_all | solution.py:50
  268.0 0.2 or_and_fusion
  268.2 37.1 %all-to-all-done = bf16[1,64,10,768]{3,2,0,1:T(8,128)(2,1)S(1)} async-done(((bf16[1,64,10,768]{3,2,0,1:T(8,128)(2,1)}), bf16[1,64,10,768]{3,2,0,1:T(8,128)(2,1)S(1)}, u32[]{:S(2)}, u32[]{:S(2)}) %all-to-all-start) | async-done | bytes 983072 | tf_op jit(solution)/shard_map/all_to_all | solution.py:50
  305.3 0.6 reshape.194
  305.9 0.7 fusion.30
  306.6 0.3 fusion.14
  306.9 0.2 fusion.32
  307.1 0.3 fusion.15
  307.4 0.3 copy.69
  307.8 1.0 reshape.196
  308.8 4.4 all-to-all-start.2
  313.4 0.9 fusion.10
  314.3 14.2 %all-to-all-done.2 = bf16[64,1,10,256]{3,2,1,0:T(8,128)(2,1)S(1)} async-done(((bf16[64,1,10,256]{3,2,1,0:T(8,128)(2,1)}), bf16[64,1,10,256]{3,2,1,0:T(8,128)(2,1)S(1)}, u32[]{:S(2)}, u32[]{:S(2)}) %all-to-all-start.2) | async-done | bytes 327712 | tf_op jit(solution)/shard_map/all_to_all | solution.py:73
  328.5 0.8 reshape.193
  329.4 68.7 %all-gather.6.cloned.1.call-done = bf16[5120,3,384]{2,0,1:T(8,128)(2,1)} async-done(((bf16[80,3,384]{2,0,1:T(8,128)(2,1)}), bf16[5120,3,384]{2,0,1:T(8,128)(2,1)}) %all-gather.6.cloned.1.call-update) | async-done | bytes 11796496 | tf_op jit(solution)/shard_map/all_gather | solution.py:46
  398.1 15.0 %copy.46 = bf16[5120,3,384]{0,2,1:T(8,128)(2,1)} copy(bf16[5120,3,384]{2,0,1:T(8,128)(2,1)} %all-gather.6.cloned.1.call-done) | data formatting | bytes 23592960 | tf_op jit(solution)/shard_map/all_gather | solution.py:46
  413.1 12.7 %convolution_convert_fusion = bf16[640,1152]{1,0:T(8,128)(2,1)S(1)} fusion(bf16[640,5120]{1,0:T(8,128)(2,1)} %all-gather.4.cloned.1.call-done, bf16[5120,1152]{0,1:T(8,128)(2,1)} %bitcast.59), kind=kOutput, calls=%fused_computation.5 | convolution fusion | flops 7550484480 | bytes 19824640 | tf_op jit(solution)/shard_map/dot_general | solution.py:44
  425.8 0.9 copy.47
  426.7 3.5 fusion.31
  430.2 4.0 fusion.12
  434.2 1.0 copy.62
  (15 shorter events, 0.5 us)
Async XLA Ops:
  7.2 119.8 %all-gather.8.cloned.1.call-start = ((), (), s32[]{:S(2)}) async-start(), calls=%async_computation.5 | async-start | bytes 7987200 | tf_op jit(solution)/shard_map/all_gather | solution.py:47
  7.9 237.4 %all-gather.4.cloned.1.call-start = ((), (), s32[]{:S(2)}) async-start(), calls=%async_computation.3 | async-start | bytes 8192000 | tf_op jit(solution)/shard_map/all_gather | solution.py:34
  8.6 389.4 %all-gather.6.cloned.1.call-start = ((), (), s32[]{:S(2)}) async-start(), calls=%async_computation.4 | async-start | bytes 11980800 | tf_op jit(solution)/shard_map/all_gather | solution.py:46
  10.9 245.6 %all-to-all-start.1 = ((bf16[1,64,10]{2,0,1:T(2,128)(2,1)}), bf16[1,64,10]{2,0,1:T(2,128)(2,1)S(1)}, u32[]{:S(2)}, u32[]{:S(2)}) async-start(bf16[1,64,10]{2,0,1:T(2,128)(2,1)} %reshape.195), calls=%async_computation.1 | async-start | bytes 65536 | tf_op jit(solution)/shard_map/all_to_all | solution.py:51
  255.0 12.9 %copy-start = (s32[1,640]{1,0:T(1,128)S(1)}, s32[1,640]{1,0:T(1,128)}, u32[]{:S(2)}) copy-start(s32[1,640]{1,0:T(1,128)} %param.8) | copy-start | bytes 7684
  256.4 48.9 %all-to-all-start = ((bf16[1,64,10,768]{3,2,0,1:T(8,128)(2,1)}), bf16[1,64,10,768]{3,2,0,1:T(8,128)(2,1)S(1)}, u32[]{:S(2)}, u32[]{:S(2)}) async-start(bf16[1,64,10,768]{3,2,0,1:T(8,128)(2,1)} %bitcast.8), calls=%async_computation | async-start | bytes 3145728 | tf_op jit(solution)/shard_map/all_to_all | solution.py:50
  305.9 7.4 %copy-start.1 = (s32[3]{0:T(128)S(1)}, s32[3]{0:T(128)}, u32[]{:S(2)}) copy-start(s32[3]{0:T(128)} %param.9) | copy-start | bytes 40
  308.8 19.7 %all-to-all-start.2 = ((bf16[64,1,10,256]{3,2,1,0:T(8,128)(2,1)}), bf16[64,1,10,256]{3,2,1,0:T(8,128)(2,1)S(1)}, u32[]{:S(2)}, u32[]{:S(2)}) async-start(bf16[64,1,10,256]{3,2,1,0:T(8,128)(2,1)} %reshape.196), calls=%async_computation.2 | async-start | bytes 1048576 | tf_op jit(solution)/shard_map/all_to_all | solution.py:73
Sparse Core Ops, SparseCore 0:
  11.5 115.4 all-gather.7
  128.8 116.4 all-gather.3
  248.8 149.2 all-gather.5
where the time goes:
time: 443 us; the launch traced here: 442 us
  waiting for transfers between devices  330 us (74%)
  local copies, waits for them, and re-layouts  33.7 us (8%)
  starting transfers between devices  31.5 us (7%)
  matrix products  30.5 us (7%)
  between operations  13.9 us (3%)
    all_gather x1, waiting for transfers between devices, body(): gathered = lax.all_gather(tokens, 'fsdp', axis=1, tiled=True)  107 us
    all_gather x1, waiting for transfers between devices, body(): acc_strided = add_rows(lax.all_gather(w_strided, 'seq', axis=0, tiled=True))  101 us
    all_gather x1, waiting for transfers between devices, body(): acc_local = add_rows(lax.all_gather(w_local, 'seq', axis=0, tiled=True))  68.7 us
    all_to_all x1, waiting for transfers between devices, body(): lax.all_to_all(packed, 'seq', split_axis=1, concat_axis=0, tiled=True)  37.1 us
    dot_general x2, matrix products, add_rows(): jnp.dot(gathered, piece.reshape(rows, -1), preferred_element_type=jnp.flo...  22.4 us
    all_to_all x1, starting transfers between devices, body(): lax.all_to_all(marks, 'seq', split_axis=1, concat_axis=0, tiled=True)  15.6 us
    all_gather x1, local copies, waits for them, and re-layouts, body(): acc_local = add_rows(lax.all_gather(w_local, 'seq', axis=0, tiled=True))  15 us
    all_to_all x1, waiting for transfers between devices, body(): lax.all_to_all(result, 'seq', split_axis=0, concat_axis=1, tiled=True)  14.2 us
  transfers between devices with their start and end apart: 6, of which 5 were waited for; matrix products, arithmetic and copies ran while one was open for 7% of the time, Pallas kernels for 0%

commit v1 on v0

--- a/solution.py
+++ b/solution.py
@@ -70,7 +70,10 @@
     probs = (expo / jnp.sum(expo, axis=-1, keepdims=True)).astype(jnp.bfloat16)
     result = jnp.einsum("shde,eshc->dshc", probs, values, preferred_element_type=jnp.float32)
     result = result.astype(jnp.bfloat16).reshape(days, 1, count, strided_cols)
-    result = lax.all_to_all(result, "seq", split_axis=0, concat_axis=1, tiled=True)
+    result = jnp.concatenate(
+        lax.all_to_all(jnp.stack(jnp.split(result, lax.axis_size("seq"), axis=0)), "seq", 0, 0),
+        axis=1,
+    )
     out_strided = result.reshape(seconds, strided_cols)
     qkv_local = acc_local.astype(jnp.bfloat16).reshape(
         seconds, 3, local_cols // head_size, head_size

time: 443 us -> 450 us (1.016)
  local copies, waits for them, and re-layouts: 33.7 us -> 73.8 us
  waiting for transfers between devices: 330 us -> 297 us
    all_gather x1, waiting for transfers between devices: 68.7 us -> 22.1 us  [body(): acc_local = add_rows(lax.all_gather(w_local, 'seq', axis=0, tiled=True))]
    unnamed x5 -> x68, local copies, waits for them, and re-layouts: 1.01 us -> 38.5 us
    all_to_all x1, waiting for transfers between devices: 14.2 us -> 27.6 us  [body(): lax.all_to_all(jnp.stack(jnp.split(result, lax.axis_size('seq'), axis=0))...]
  transfers between devices with their start and end apart: 6 -> 6, of which waited for: 5 -> 5; matrix products, arithmetic and copies ran while one was open for 7% -> 15% of each run, Pallas kernels for 0% -> 0%
where the time goes in v1:
time: 450 us; the launch traced here: 449 us
  waiting for transfers between devices  297 us (66%)
  local copies, waits for them, and re-layouts  73.8 us (16%)
  starting transfers between devices  31.5 us (7%)
  matrix products  30.5 us (7%)
  between operations  14.1 us (3%)
    all_gather x1, waiting for transfers between devices, body(): gathered = lax.all_gather(tokens, 'fsdp', axis=1, tiled=True)  107 us
    all_gather x1, waiting for transfers between devices, body(): acc_strided = add_rows(lax.all_gather(w_strided, 'seq', axis=0, tiled=True))  101 us
    unnamed x68, local copies, waits for them, and re-layouts  38.5 us
    all_to_all x1, waiting for transfers between devices, body(): lax.all_to_all(packed, 'seq', split_axis=1, concat_axis=0, tiled=True)  37.1 us
    all_to_all x1, waiting for transfers between devices, body(): lax.all_to_all(jnp.stack(jnp.split(result, lax.axis_size('seq'), axis=0))...  27.6 us
    dot_general x2, matrix products, add_rows(): jnp.dot(gathered, piece.reshape(rows, -1), preferred_element_type=jnp.flo...  22.4 us
    all_gather x1, waiting for transfers between devices, body(): acc_local = add_rows(lax.all_gather(w_local, 'seq', axis=0, tiled=True))  22.1 us
    all_to_all x1, starting transfers between devices, body(): lax.all_to_all(marks, 'seq', split_axis=1, concat_axis=0, tiled=True)  15.6 us
  transfers between devices with their start and end apart: 6, of which 5 were waited for; matrix products, arithmetic and copies ran while one was open for 15% of the time, Pallas kernels for 0%

profile of v1, /device:TPU:1, one launch (start us, length us, event | category | flops | bytes accessed | tf_op | source)
XLA Modules:
  0.0 448.7 jit_solution(4240641726672757323)
XLA Ops:
  7.2 0.7 all-gather.8.cloned.1.call-update
  7.9 0.7 all-gather.4.cloned.1.call-update
  8.7 0.7 all-gather.6.cloned.1.call-update
  9.4 0.7 convert_reduce_fusion
  10.1 0.8 reshape.312
  10.9 15.6 %all-to-all-start.1 = ((bf16[1,64,10]{2,0,1:T(2,128)(2,1)}), bf16[1,64,10]{2,0,1:T(2,128)(2,1)S(1)}, u32[]{:S(2)}, u32[]{:S(2)}) async-start(bf16[1,64,10]{2,0,1:T(2,128)(2,1)} %reshape.312), calls=%async_computation.1 | async-start | bytes 65536 | tf_op jit(solution)/shard_map/all_to_all | solution.py:51
  26.5 100.5 %all-gather.8.cloned.1.call-done = bf16[5120,3,256]{2,0,1:T(8,128)(2,1)} async-done(((bf16[80,3,256]{2,0,1:T(8,128)(2,1)}), bf16[5120,3,256]{2,0,1:T(8,128)(2,1)}) %all-gather.8.cloned.1.call-update) | async-done | bytes 7864336 | tf_op jit(solution)/shard_map/all_gather | solution.py:47
  127.0 11.0 %copy.47 = bf16[5120,3,256]{0,2,1:T(8,128)(2,1)} copy(bf16[5120,3,256]{2,0,1:T(8,128)(2,1)} %all-gather.8.cloned.1.call-done) | data formatting | bytes 15728640 | tf_op jit(solution)/shard_map/all_gather | solution.py:47
  138.0 107.3 %all-gather.4.cloned.1.call-done = bf16[640,5120]{1,0:T(8,128)(2,1)} async-done(((bf16[640,1280]{1,0:T(8,128)(2,1)}), bf16[640,5120]{1,0:T(8,128)(2,1)}) %all-gather.4.cloned.1.call-update) | async-done | bytes 6553616 | tf_op jit(solution)/shard_map/all_gather | solution.py:34
  245.3 9.7 %convolution_convert_fusion.1 = bf16[640,768]{1,0:T(8,128)(2,1)S(1)} fusion(bf16[640,5120]{1,0:T(8,128)(2,1)} %all-gather.4.cloned.1.call-done, bf16[5120,768]{0,1:T(8,128)(2,1)} %bitcast.60), kind=kOutput, calls=%fused_computation.17 | convolution fusion | flops 5033656320 | bytes 15400960 | tf_op jit(solution)/shard_map/dot_general | solution.py:44
  255.0 1.4 reshape.308
  256.4 11.4 %all-to-all-start = ((bf16[1,64,10,768]{3,2,0,1:T(8,128)(2,1)}), bf16[1,64,10,768]{3,2,0,1:T(8,128)(2,1)S(1)}, u32[]{:S(2)}, u32[]{:S(2)}) async-start(bf16[1,64,10,768]{3,2,0,1:T(8,128)(2,1)} %bitcast.8), calls=%async_computation | async-start | bytes 3145728 | tf_op jit(solution)/shard_map/all_to_all | solution.py:50
  268.2 37.1 %all-to-all-done = bf16[1,64,10,768]{3,2,0,1:T(8,128)(2,1)S(1)} async-done(((bf16[1,64,10,768]{3,2,0,1:T(8,128)(2,1)}), bf16[1,64,10,768]{3,2,0,1:T(8,128)(2,1)S(1)}, u32[]{:S(2)}, u32[]{:S(2)}) %all-to-all-start) | async-done | bytes 983072 | tf_op jit(solution)/shard_map/all_to_all | solution.py:50
  305.9 0.7 fusion.30
  307.8 0.6 slice_reduce_fusion.38
  308.8 0.6 slice_reduce_fusion
  309.5 0.6 slice_reduce_fusion.19
  322.8 0.6 constant_dynamic-update-slice_fusion.43
  333.0 0.6 constant_dynamic-update-slice_fusion.26
  337.1 0.6 constant_dynamic-update-slice_fusion.19
  342.5 0.6 constant_dynamic-update-slice_fusion.10
  349.0 4.4 all-to-all-start.2
  353.7 0.9 fusion.10
  354.6 27.6 %all-to-all-done.2 = bf16[64,1,1,10,256]{4,3,2,1,0:T(8,128)(2,1)S(1)} async-done(((bf16[64,1,1,10,256]{4,3,2,1,0:T(8,128)(2,1)}), bf16[64,1,1,10,256]{4,3,2,1,0:T(8,128)(2,1)S(1)}, u32[]{:S(2)}, u32[]{:S(2)}) %all-to-all-start.2) | async-done | bytes 327712 | tf_op jit(solution)/shard_map/all_to_all | solution.py:74
  382.2 0.8 reshape_reshape.3
  383.0 22.1 %all-gather.6.cloned.1.call-done = bf16[5120,3,384]{2,0,1:T(8,128)(2,1)} async-done(((bf16[80,3,384]{2,0,1:T(8,128)(2,1)}), bf16[5120,3,384]{2,0,1:T(8,128)(2,1)}) %all-gather.6.cloned.1.call-update) | async-done | bytes 11796496 | tf_op jit(solution)/shard_map/all_gather | solution.py:46
  405.1 15.0 %copy.42 = bf16[5120,3,384]{0,2,1:T(8,128)(2,1)} copy(bf16[5120,3,384]{2,0,1:T(8,128)(2,1)} %all-gather.6.cloned.1.call-done) | data formatting | bytes 23592960 | tf_op jit(solution)/shard_map/all_gather | solution.py:46
  420.1 12.7 %convolution_convert_fusion = bf16[640,1152]{1,0:T(8,128)(2,1)S(1)} fusion(bf16[640,5120]{1,0:T(8,128)(2,1)} %all-gather.4.cloned.1.call-done, bf16[5120,1152]{0,1:T(8,128)(2,1)} %bitcast.59), kind=kOutput, calls=%fused_computation.5 | convolution fusion | flops 7550484480 | bytes 19824640 | tf_op jit(solution)/shard_map/dot_general | solution.py:44
  432.8 0.9 copy.43
  433.7 3.5 fusion.31
  437.2 4.0 fusion.12
  441.2 1.0 copy.56
  (145 shorter events, 39.2 us)
Async XLA Ops:
  7.2 119.8 %all-gather.8.cloned.1.call-start = ((), (), s32[]{:S(2)}) async-start(), calls=%async_computation.5 | async-start | bytes 7987200 | tf_op jit(solution)/shard_map/all_gather | solution.py:47
  7.9 237.4 %all-gather.4.cloned.1.call-start = ((), (), s32[]{:S(2)}) async-start(), calls=%async_computation.3 | async-start | bytes 8192000 | tf_op jit(solution)/shard_map/all_gather | solution.py:34
  8.6 396.4 %all-gather.6.cloned.1.call-start = ((), (), s32[]{:S(2)}) async-start(), calls=%async_computation.4 | async-start | bytes 11980800 | tf_op jit(solution)/shard_map/all_gather | solution.py:46
  10.9 245.6 %all-to-all-start.1 = ((bf16[1,64,10]{2,0,1:T(2,128)(2,1)}), bf16[1,64,10]{2,0,1:T(2,128)(2,1)S(1)}, u32[]{:S(2)}, u32[]{:S(2)}) async-start(bf16[1,64,10]{2,0,1:T(2,128)(2,1)} %reshape.312), calls=%async_computation.1 | async-start | bytes 65536 | tf_op jit(solution)/shard_map/all_to_all | solution.py:51
  255.0 12.9 %copy-start = (s32[1,640]{1,0:T(1,128)S(1)}, s32[1,640]{1,0:T(1,128)}, u32[]{:S(2)}) copy-start(s32[1,640]{1,0:T(1,128)} %param.8) | copy-start | bytes 7684
  256.4 48.9 %all-to-all-start = ((bf16[1,64,10,768]{3,2,0,1:T(8,128)(2,1)}), bf16[1,64,10,768]{3,2,0,1:T(8,128)(2,1)S(1)}, u32[]{:S(2)}, u32[]{:S(2)}) async-start(bf16[1,64,10,768]{3,2,0,1:T(8,128)(2,1)} %bitcast.8), calls=%async_computation | async-start | bytes 3145728 | tf_op jit(solution)/shard_map/all_to_all | solution.py:50
  306.6 47.0 %copy-start.1 = (s32[3]{0:T(128)S(1)}, s32[3]{0:T(128)}, u32[]{:S(2)}) copy-start(s32[3]{0:T(128)} %param.9) | copy-start | bytes 40
  349.0 33.1 %all-to-all-start.2 = ((bf16[64,1,1,10,256]{4,3,2,1,0:T(8,128)(2,1)}), bf16[64,1,1,10,256]{4,3,2,1,0:T(8,128)(2,1)S(1)}, u32[]{:S(2)}, u32[]{:S(2)}) async-start(bf16[64,1,1,10,256]{4,3,2,1,0:T(8,128)(2,1)} %constant_dynamic-update-slice_fusion), calls=%async_computation.2 | async-start | bytes 1048576 | tf_op jit(solution)/shard_map/all_to_all | solution.py:74
Sparse Core Ops, SparseCore 0:
  11.5 115.4 all-gather.7
  128.8 116.4 all-gather.3
  248.8 156.2 all-gather.5
